TPU v7x, 256 devices: a whole 4x4x8 slice. The times are simulated.
256 devices in a mesh: row: 16 (over z, core), col: 16 (over y, x).
Axes of the slice: x: 4, y: 4, z: 8, core: 2. Of those that a mesh axis runs over, the one named last changes fastest.
Arguments:
- rhs: float32 [24576, 12288], P('row', 'col'), may hold values from -6 to 6
- panels_l: float32 [4, 24576, 512], P(None, 'row', 'col'), may hold values from -0.25 to 0.25
- diag_inverse: float32 [4, 512, 512], P(None, None, 'col'), may hold values from -1.5 to 1.5, as said below
Outputs:
- solved_rhs: float32 [24576, 12288], P('row', 'col')
Inputs may be any that keep to these rules, and one draw needn't show every extreme that they name: `diag_inverse`: each tile is lower triangular with diagonal entries between 0.5 and 1.5.
All inputs are finite; a program needn't handle non-finite values.
Results may differ from a plain program's by a relative error of at most 0.00016.
Values sent between devices are 32-bit elements; how exact they have to be, the bound alone decides.
A program may use at most 128 MiB of HBM per device.

v0:
```python
import jax
import jax.numpy as jnp
from jax import lax
from jax.sharding import PartitionSpec as P


def spread(x, axis, root):
    mine = lax.axis_index(axis) == root
    return lax.psum(jnp.where(mine, x, jnp.zeros_like(x)), axis)


def exact_dot(left, right):
    return jnp.dot(left, right, precision=lax.Precision.HIGHEST, preferred_element_type=jnp.float32)


def per_device(rhs, panels_l, diag_inverse):
    rows_here = rhs.shape[0]
    width = diag_inverse.shape[1]
    count = panels_l.shape[0]
    my_row = lax.axis_index("row")
    global_rows = my_row * rows_here + lax.iota(jnp.int32, rows_here)
    work = rhs
    for k in range(count):
        factor_cols = lax.all_gather(panels_l[k], "col", axis=1, tiled=True)
        inverse_tile = lax.all_gather(diag_inverse[k], "col", axis=1, tiled=True)
        owner = k * width // rows_here
        offset = k * width - owner * rows_here
        strip = work[offset : offset + width]
        is_owner = my_row == owner
        solved_here = lax.cond(
            is_owner,
            lambda: exact_dot(inverse_tile, strip),
            lambda: jnp.zeros(strip.shape, jnp.float32),
        )
        solved = spread(solved_here, "row", owner)
        update = exact_dot(factor_cols, solved)
        below = (global_rows >= (k + 1) * width)[:, None]
        work = jnp.where(below, work - update, work)
        work = work.at[offset : offset + width].set(
            jnp.where(is_owner, solved, work[offset : offset + width])
        )
    return work


def solution(mesh):
    in_specs = (P("row", "col"), P(None, "row", "col"), P(None, None, "col"))
    out_specs = P("row", "col")
    return jax.shard_map(
        per_device, mesh=mesh, in_specs=in_specs, out_specs=out_specs, check_vma=False
    )
```

profile of v0, /device:TPU:1, one launch (start us, length us, event | category | flops | bytes accessed | tf_op | source)
XLA Modules:
  0.0 919.6 jit_solution(2855108133627082533)
XLA Ops:
  6.5 1.0 fusion.27
  8.3 51.0 %all-gather.17.cloned.1.call-done = f32[1,512,512]{1,0,2:T(1,128)} async-done(((f32[1,512,32]{1,0,2:T(1,128)}), f32[1,512,512]{1,0,2:T(1,128)}) %all-gather.17.cloned.1.call-update) | async-done | bytes 1048592 | tf_op jit(solution)/shard_map/all_gather | solution.py:25
  59.3 1.3 copy.69
  60.8 1.4 broadcast_select_fusion.3
  62.2 1.1 copy-done.7
  65.6 6.0 copy.21
  71.7 105.5 %all-reduce.5.cloned.1.call-done = f32[512,768]{0,1:T(8,128)} async-done(((f32[512,768]{0,1:T(8,128)}), f32[512,768]{0,1:T(8,128)}) %all-reduce.5.cloned.1.call-update) | async-done | bytes 1572880 | tf_op jit(solution)/shard_map/psum | solution.py:9
  177.2 55.1 %all-gather.19.cloned.1.call-done = f32[1,1536,512]{1,2,0:T(8,128)} async-done(((f32[1,1536,32]{1,2,0:T(8,128)}), f32[1,1536,512]{1,2,0:T(8,128)}) %all-gather.19.cloned.1.call-update) | async-done | bytes 3145744 | tf_op jit(solution)/shard_map/all_gather | solution.py:24
  232.3 12.0 %subtract_select_fusion.3 = f32[1536,768]{0,1:T(8,128)} fusion(f32[1536,768]{0,1:T(8,128)} %copy.21, f32[512,768]{0,1:T(8,128)} %all-reduce.5.cloned.1.call-done, f32[1,1536,512]{1,2,0:T(8,128)} %all-gather.19.cloned.1.call-done, pred[1536]{0:T(1024)(128)(4,1)S(1)} %fusion.22), kind=kOutput, calls=%fused_computation.17 | convolution fusion | flops 7250116608 | bytes 14157312 | tf_op jit(solution)/shard_map/dot_general | solution.py:13
  244.3 2.9 fusion.21
  247.2 32.6 %all-gather.21.cloned.1.call-done = f32[1,512,512]{1,0,2:T(1,128)} async-done(((f32[1,512,32]{1,0,2:T(1,128)}), f32[1,512,512]{1,0,2:T(1,128)}) %all-gather.21.cloned.1.call-update) | async-done | bytes 1048592 | tf_op jit(solution)/shard_map/all_gather | solution.py:25
  280.2 1.3 broadcast_select_fusion.2
  283.1 52.3 %all-gather.23.cloned.1.call-done = f32[1,1536,512]{1,2,0:T(8,128)} async-done(((f32[1,1536,32]{1,2,0:T(8,128)}), f32[1,1536,512]{1,2,0:T(8,128)}) %all-gather.23.cloned.1.call-update) | async-done | bytes 3145744 | tf_op jit(solution)/shard_map/all_gather | solution.py:24
  335.5 115.4 %all-reduce.7.cloned.1.call-done = f32[512,768]{0,1:T(8,128)} async-done(((f32[512,768]{0,1:T(8,128)}), f32[512,768]{0,1:T(8,128)}) %all-reduce.7.cloned.1.call-update) | async-done | bytes 1572880 | tf_op jit(solution)/shard_map/psum | solution.py:9
  450.9 12.9 %subtract_select_fusion.2 = f32[1536,768]{0,1:T(8,128)} fusion(f32[1536,768]{0,1:T(8,128)} %fusion.21, f32[512,768]{0,1:T(8,128)} %all-reduce.7.cloned.1.call-done, f32[1,1536,512]{1,2,0:T(8,128)} %all-gather.23.cloned.1.call-done, pred[1536]{0:T(1024)(128)(4,1)S(1)} %fusion.23), kind=kOutput, calls=%fused_computation.16 | convolution fusion | flops 7250116608 | bytes 14157312 | tf_op jit(solution)/shard_map/dot_general | solution.py:13
  463.8 2.9 fusion.20
  466.7 32.8 %all-gather.25.cloned.1.call-done = f32[1,512,512]{1,0,2:T(1,128)} async-done(((f32[1,512,32]{1,0,2:T(1,128)}), f32[1,512,512]{1,0,2:T(1,128)}) %all-gather.25.cloned.1.call-update) | async-done | bytes 1048592 | tf_op jit(solution)/shard_map/all_gather | solution.py:25
  499.7 1.3 broadcast_select_fusion.1
  502.8 52.5 %all-gather.27.cloned.1.call-done = f32[1,1536,512]{1,2,0:T(8,128)} async-done(((f32[1,1536,32]{1,2,0:T(8,128)}), f32[1,1536,512]{1,2,0:T(8,128)}) %all-gather.27.cloned.1.call-update) | async-done | bytes 3145744 | tf_op jit(solution)/shard_map/all_gather | solution.py:24
  555.3 115.6 %all-reduce.9.cloned.1.call-done = f32[512,768]{0,1:T(8,128)} async-done(((f32[512,768]{0,1:T(8,128)}), f32[512,768]{0,1:T(8,128)}) %all-reduce.9.cloned.1.call-update) | async-done | bytes 1572880 | tf_op jit(solution)/shard_map/psum | solution.py:9
  670.9 12.9 %subtract_select_fusion.1 = f32[1536,768]{0,1:T(8,128)} fusion(f32[1536,768]{0,1:T(8,128)} %fusion.20, f32[512,768]{0,1:T(8,128)} %all-reduce.9.cloned.1.call-done, f32[1,1536,512]{1,2,0:T(8,128)} %all-gather.27.cloned.1.call-done, pred[1536]{0:T(1024)(128)(4,1)S(1)} %fusion.24), kind=kOutput, calls=%fused_computation.15 | convolution fusion | flops 7250116608 | bytes 14157312 | tf_op jit(solution)/shard_map/dot_general | solution.py:13
  683.8 2.9 fusion.19
  686.7 32.7 %all-gather.29.cloned.1.call-done = f32[1,512,512]{1,0,2:T(1,128)} async-done(((f32[1,512,32]{1,0,2:T(1,128)}), f32[1,512,512]{1,0,2:T(1,128)}) %all-gather.29.cloned.1.call-update) | async-done | bytes 1048592 | tf_op jit(solution)/shard_map/all_gather | solution.py:25
  719.4 10.5 %conditional.7 = (f32[512,768]{0,1:T(8,128)S(1)}) conditional(s32[]{:T(128)} %convert_element_type.9, () %tuple.51, (f32[1536,768]{0,1:T(8,128)}, f32[1,512,512]{1,0,2:T(1,128)}) %tuple.52), branch_computations={%region_9.10_spmd, %region_10.11_spmd} | conditional | flops 2415919104 | bytes 17825828 | solution.py:30
  719.4 6.1 copy.32
  725.5 4.1 fusion.10
  729.8 1.3 broadcast_select_fusion
  731.2 44.0 %all-gather.31.cloned.1.call-done = f32[1,1536,512]{1,2,0:T(8,128)} async-done(((f32[1,1536,32]{1,2,0:T(8,128)}), f32[1,1536,512]{1,2,0:T(8,128)}) %all-gather.31.cloned.1.call-update) | async-done | bytes 3145744 | tf_op jit(solution)/shard_map/all_gather | solution.py:24
  775.2 115.4 %all-reduce.11.cloned.1.call-done = f32[512,768]{0,1:T(8,128)} async-done(((f32[512,768]{0,1:T(8,128)}), f32[512,768]{0,1:T(8,128)}) %all-reduce.11.cloned.1.call-update) | async-done | bytes 1572880 | tf_op jit(solution)/shard_map/psum | solution.py:9
  890.6 13.1 %subtract_select_fusion = f32[1536,768]{0,1:T(8,128)} fusion(f32[1536,768]{0,1:T(8,128)} %fusion.19, f32[512,768]{0,1:T(8,128)} %all-reduce.11.cloned.1.call-done, f32[1,1536,512]{1,2,0:T(8,128)} %all-gather.31.cloned.1.call-done, pred[1536]{0:T(1024)(128)(4,1)S(1)} %fusion.25), kind=kOutput, calls=%fused_computation.14 | convolution fusion | flops 7250116608 | bytes 14157312 | tf_op jit(solution)/shard_map/dot_general | solution.py:13
  903.6 3.0 fusion.18
  906.7 6.0 copy.35
  (50 shorter events, 7.8 us)
Async XLA Ops:
  6.5 52.8 %all-gather.17.cloned.1.call-start = ((), (), s32[]{:S(2)}) async-start(), calls=%async_computation.4 | async-start | bytes 1114112 | tf_op jit(solution)/shard_map/all_gather | solution.py:25
  8.2 169.0 %all-reduce.5.cloned.1.call-start = ((), (), s32[]{:S(2)}) async-start(), calls=%async_computation | async-start | bytes 3145728 | tf_op jit(solution)/shard_map/psum | solution.py:9
  62.2 1.1 copy-start.7
  62.2 170.2 %all-gather.19.cloned.1.call-start = ((), (), s32[]{:S(2)}) async-start(), calls=%async_computation.5 | async-start | bytes 3342336 | tf_op jit(solution)/shard_map/all_gather | solution.py:24
  64.2 215.6 %all-gather.21.cloned.1.call-start = ((), (), s32[]{:S(2)}) async-start(), calls=%async_computation.6 | async-start | bytes 1114112 | tf_op jit(solution)/shard_map/all_gather | solution.py:25
  65.0 270.5 %all-gather.23.cloned.1.call-start = ((), (), s32[]{:S(2)}) async-start(), calls=%async_computation.7 | async-start | bytes 3342336 | tf_op jit(solution)/shard_map/all_gather | solution.py:24
  65.6 385.3 %all-reduce.7.cloned.1.call-start = ((), (), s32[]{:S(2)}) async-start(), calls=%async_computation.1 | async-start | bytes 3145728 | tf_op jit(solution)/shard_map/psum | solution.py:9
  177.2 67.1 %copy-start = (f32[512,768]{0,1:T(8,128)S(1)}, f32[512,768]{0,1:T(8,128)}, u32[]{:S(2)}) copy-start(f32[512,768]{0,1:T(8,128)} %all-reduce.5.cloned.1.call-done) | copy-start | bytes 4718596
  281.5 218.0 %all-gather.25.cloned.1.call-start = ((), (), s32[]{:S(2)}) async-start(), calls=%async_computation.8 | async-start | bytes 1114112 | tf_op jit(solution)/shard_map/all_gather | solution.py:25
  282.3 273.0 %all-gather.27.cloned.1.call-start = ((), (), s32[]{:S(2)}) async-start(), calls=%async_computation.9 | async-start | bytes 3342336 | tf_op jit(solution)/shard_map/all_gather | solution.py:24
  283.0 387.8 %all-reduce.9.cloned.1.call-start = ((), (), s32[]{:S(2)}) async-start(), calls=%async_computation.2 | async-start | bytes 3145728 | tf_op jit(solution)/shard_map/psum | solution.py:9
  450.9 12.9 %copy-start.2 = (f32[512,768]{0,1:T(8,128)S(1)}, f32[512,768]{0,1:T(8,128)}, u32[]{:S(2)}) copy-start(f32[512,768]{0,1:T(8,128)} %all-reduce.7.cloned.1.call-done) | copy-start | bytes 4718596
  501.1 218.3 %all-gather.29.cloned.1.call-start = ((), (), s32[]{:S(2)}) async-start(), calls=%async_computation.10 | async-start | bytes 1114112 | tf_op jit(solution)/shard_map/all_gather | solution.py:25
  501.8 273.4 %all-gather.31.cloned.1.call-start = ((), (), s32[]{:S(2)}) async-start(), calls=%async_computation.11 | async-start | bytes 3342336 | tf_op jit(solution)/shard_map/all_gather | solution.py:24
  502.6 388.0 %all-reduce.11.cloned.1.call-start = ((), (), s32[]{:S(2)}) async-start(), calls=%async_computation.3 | async-start | bytes 3145728 | tf_op jit(solution)/shard_map/psum | solution.py:9
  670.9 12.9 %copy-start.1 = (f32[512,768]{0,1:T(8,128)S(1)}, f32[512,768]{0,1:T(8,128)}, u32[]{:S(2)}) copy-start(f32[512,768]{0,1:T(8,128)} %all-reduce.9.cloned.1.call-done) | copy-start | bytes 4718596
  719.4 6.1 copy-start.4
  890.6 13.1 %copy-start.3 = (f32[512,768]{0,1:T(8,128)S(1)}, f32[512,768]{0,1:T(8,128)}, u32[]{:S(2)}) copy-start(f32[512,768]{0,1:T(8,128)} %all-reduce.11.cloned.1.call-done) | copy-start | bytes 4718596
Sparse Core Ops, SparseCore 0:
  9.8 49.4 all-gather.16
  62.3 114.8 all-reduce.4
  179.7 52.6 all-gather.18
  234.6 45.1 all-gather.20
  282.1 53.3 all-gather.22
  337.7 113.1 all-reduce.6
  453.3 46.1 all-gather.24
  501.9 53.3 all-gather.26
  557.7 113.1 all-reduce.8
  673.2 46.1 all-gather.28
  721.8 53.3 all-gather.30
  777.4 113.1 all-reduce.10
where the time goes:
time: 920 us
  waiting for transfers between devices  807 us (88%)
  matrix products  54.9 us (6%)
  local copies, waits for them, and re-layouts  25.7 us (3%)
  other arithmetic  17.1 us (2%)
  between operations  13.7 us (1%)
    psum x4, waiting for transfers between devices, spread(): return lax.psum(jnp.where(mine, x, jnp.zeros_like(x)), axis)  452 us
    all_gather x4, waiting for transfers between devices, per_device(): factor_cols = lax.all_gather(panels_l[k], 'col', axis=1, tiled=True)  204 us
    all_gather x4, waiting for transfers between devices, per_device(): inverse_tile = lax.all_gather(diag_inverse[k], 'col', axis=1, tiled=True)  149 us
    dot_general x4, matrix products, exact_dot(): jnp.dot(left, right, precision=lax.Precision.HIGHEST, preferred_element_t...  50.9 us
  transfers between devices with their start and end apart: 12, of which 12 were waited for; matrix products, arithmetic and copies ran while one was open for 8% of the time, Pallas kernels for 0%

commit v1 on v0

--- a/solution.py
+++ b/solution.py
@@ -6,7 +6,7 @@
 
 def spread(x, axis, root):
     mine = lax.axis_index(axis) == root
-    return lax.psum(jnp.where(mine, x, jnp.zeros_like(x)), axis)
+    return jnp.sum(lax.all_gather(jnp.where(mine, x, jnp.zeros_like(x)), axis), axis=0)
 
 
 def exact_dot(left, right):

time: 920 us -> 1010 us (1.098)
  local copies, waits for them, and re-layouts: 25.7 us -> 133 us
  waiting for transfers between devices: 807 us -> 767 us
  other arithmetic: 17.1 us -> 42.3 us
    all_gather x0 -> x4, waiting for transfers between devices: none -> 536 us  [spread(): lax.all_gather(jnp.where(mine, x, jnp.zeros_like(x)), axis)]
    psum x4 -> x0, waiting for transfers between devices: 452 us -> none  [spread(): return lax.psum(jnp.where(mine, x, jnp.zeros_like(x)), axis)]
    all_gather x4, waiting for transfers between devices: 204 us -> 78.7 us  [per_device(): factor_cols = lax.all_gather(panels_l[k], 'col', axis=1, tiled=True)]
    unnamed x16 -> x12, local copies, waits for them, and re-layouts: 11.2 us -> 118 us
    reduce_sum x0 -> x4, other arithmetic: none -> 25.2 us  [spread(): jnp.sum(lax.all_gather(jnp.where(mine, x, jnp.zeros_like(x)), axis), axis=0)]
  transfers between devices with their start and end apart: 12 -> 12, of which waited for: 12 -> 12; matrix products, arithmetic and copies ran while one was open for 8% -> 18% of each run, Pallas kernels for 0% -> 0%
where the time goes in v1:
time: 1010 us
  waiting for transfers between devices  767 us (76%)
  local copies, waits for them, and re-layouts  133 us (13%)
  matrix products  50.3 us (5%)
  other arithmetic  42.3 us (4%)
  between operations  13.9 us (1%)
    all_gather x4, waiting for transfers between devices, spread(): lax.all_gather(jnp.where(mine, x, jnp.zeros_like(x)), axis)  536 us
    all_gather x4, waiting for transfers between devices, per_device(): inverse_tile = lax.all_gather(diag_inverse[k], 'col', axis=1, tiled=True)  150 us
    unnamed x12, local copies, waits for them, and re-layouts  118 us
    all_gather x4, waiting for transfers between devices, per_device(): factor_cols = lax.all_gather(panels_l[k], 'col', axis=1, tiled=True)  78.7 us
    dot_general x4, matrix products, exact_dot(): jnp.dot(left, right, precision=lax.Precision.HIGHEST, preferred_element_t...  46.2 us
    reduce_sum x4, other arithmetic, spread(): jnp.sum(lax.all_gather(jnp.where(mine, x, jnp.zeros_like(x)), axis), axis=0)  25.2 us
  transfers between devices with their start and end apart: 12, of which 12 were waited for; matrix products, arithmetic and copies ran while one was open for 18% of the time, Pallas kernels for 0%

profile of v1, /device:TPU:1, one launch (start us, length us, event | category | flops | bytes accessed | tf_op | source)
XLA Modules:
  0.0 1007.2 jit_solution(10903538633584687298)
XLA Ops:
  8.3 51.0 %all-gather.25.cloned.1.call-done = f32[1,512,512]{1,0,2:T(1,128)} async-done(((f32[1,512,32]{1,0,2:T(1,128)}), f32[1,512,512]{1,0,2:T(1,128)}) %all-gather.25.cloned.1.call-update) | async-done | bytes 1048592 | tf_op jit(solution)/shard_map/all_gather | solution.py:25
  65.3 6.0 copy.21
  71.3 127.5 %all-gather.27.cloned.1.call-done = f32[8192,768]{0,1:T(8,128)} async-done(((f32[512,768]{0,1:T(8,128)}), f32[8192,768]{0,1:T(8,128)}) %all-gather.27.cloned.1.call-update) | async-done | bytes 25165840 | tf_op jit(solution)/shard_map/all_gather | solution.py:9
  198.8 26.7 %copy.56 = f32[96,8,16,512]{3,2,1,0:T(8,128)S(1)} copy(f32[96,8,16,512]{3,1,2,0:T(8,128)} %bitcast.57) | data formatting | bytes 50331648
  225.5 6.3 bitcast_reduce_fusion.3
  231.8 19.7 %all-gather.29.cloned.1.call-done = f32[1,1536,512]{1,2,0:T(8,128)} async-done(((f32[1,1536,32]{1,2,0:T(8,128)}), f32[1,1536,512]{1,2,0:T(8,128)}) %all-gather.29.cloned.1.call-update) | async-done | bytes 3145744 | tf_op jit(solution)/shard_map/all_gather | solution.py:24
  251.6 11.5 %subtract_select_fusion.3 = f32[1536,768]{0,1:T(8,128)} fusion(f32[1536,768]{0,1:T(8,128)} %copy.21, f32[512,768]{0,1:T(8,128)S(1)} %bitcast_reduce_fusion.3, f32[1,1536,512]{1,2,0:T(8,128)} %all-gather.29.cloned.1.call-done, pred[1536]{0:T(1024)(128)(4,1)S(1)} %fusion.22), kind=kOutput, calls=%fused_computation.21 | convolution fusion | flops 7250116608 | bytes 14157312 | tf_op jit(solution)/shard_map/dot_general | solution.py:13
  263.1 2.9 fusion.21
  266.0 33.0 %all-gather.31.cloned.1.call-done = f32[1,512,512]{1,0,2:T(1,128)} async-done(((f32[1,512,32]{1,0,2:T(1,128)}), f32[1,512,512]{1,0,2:T(1,128)}) %all-gather.31.cloned.1.call-update) | async-done | bytes 1048592 | tf_op jit(solution)/shard_map/all_gather | solution.py:25
  302.4 140.1 %all-gather.33.cloned.1.call-done = f32[8192,768]{0,1:T(8,128)} async-done(((f32[512,768]{0,1:T(8,128)}), f32[8192,768]{0,1:T(8,128)}) %all-gather.33.cloned.1.call-update) | async-done | bytes 25165840 | tf_op jit(solution)/shard_map/all_gather | solution.py:9
  442.5 26.7 %copy.57 = f32[96,8,16,512]{3,2,1,0:T(8,128)S(1)} copy(f32[96,8,16,512]{3,1,2,0:T(8,128)} %bitcast.59) | data formatting | bytes 50331648
  469.2 6.3 bitcast_reduce_fusion.2
  475.5 19.6 %all-gather.35.cloned.1.call-done = f32[1,1536,512]{1,2,0:T(8,128)} async-done(((f32[1,1536,32]{1,2,0:T(8,128)}), f32[1,1536,512]{1,2,0:T(8,128)}) %all-gather.35.cloned.1.call-update) | async-done | bytes 3145744 | tf_op jit(solution)/shard_map/all_gather | solution.py:24
  495.1 11.5 %subtract_select_fusion.2 = f32[1536,768]{0,1:T(8,128)} fusion(f32[1536,768]{0,1:T(8,128)} %fusion.21, f32[512,768]{0,1:T(8,128)S(1)} %bitcast_reduce_fusion.2, f32[1,1536,512]{1,2,0:T(8,128)} %all-gather.35.cloned.1.call-done, pred[1536]{0:T(1024)(128)(4,1)S(1)} %fusion.23), kind=kOutput, calls=%fused_computation.20 | convolution fusion | flops 7250116608 | bytes 14157312 | tf_op jit(solution)/shard_map/dot_general | solution.py:13
  506.6 2.9 fusion.20
  509.5 33.2 %all-gather.37.cloned.1.call-done = f32[1,512,512]{1,0,2:T(1,128)} async-done(((f32[1,512,32]{1,0,2:T(1,128)}), f32[1,512,512]{1,0,2:T(1,128)}) %all-gather.37.cloned.1.call-update) | async-done | bytes 1048592 | tf_op jit(solution)/shard_map/all_gather | solution.py:25
  546.1 139.9 %all-gather.39.cloned.1.call-done = f32[8192,768]{0,1:T(8,128)} async-done(((f32[512,768]{0,1:T(8,128)}), f32[8192,768]{0,1:T(8,128)}) %all-gather.39.cloned.1.call-update) | async-done | bytes 25165840 | tf_op jit(solution)/shard_map/all_gather | solution.py:9
  686.0 26.7 %copy.58 = f32[96,8,16,512]{3,2,1,0:T(8,128)S(1)} copy(f32[96,8,16,512]{3,1,2,0:T(8,128)} %bitcast.58) | data formatting | bytes 50331648
  712.7 6.3 bitcast_reduce_fusion.1
  719.0 19.7 %all-gather.41.cloned.1.call-done = f32[1,1536,512]{1,2,0:T(8,128)} async-done(((f32[1,1536,32]{1,2,0:T(8,128)}), f32[1,1536,512]{1,2,0:T(8,128)}) %all-gather.41.cloned.1.call-update) | async-done | bytes 3145744 | tf_op jit(solution)/shard_map/all_gather | solution.py:24
  738.7 11.5 %subtract_select_fusion.1 = f32[1536,768]{0,1:T(8,128)} fusion(f32[1536,768]{0,1:T(8,128)} %fusion.20, f32[512,768]{0,1:T(8,128)S(1)} %bitcast_reduce_fusion.1, f32[1,1536,512]{1,2,0:T(8,128)} %all-gather.41.cloned.1.call-done, pred[1536]{0:T(1024)(128)(4,1)S(1)} %fusion.24), kind=kOutput, calls=%fused_computation.19 | convolution fusion | flops 7250116608 | bytes 14157312 | tf_op jit(solution)/shard_map/dot_general | solution.py:13
  753.1 33.0 %all-gather.43.cloned.1.call-done = f32[1,512,512]{1,0,2:T(1,128)} async-done(((f32[1,512,32]{1,0,2:T(1,128)}), f32[1,512,512]{1,0,2:T(1,128)}) %all-gather.43.cloned.1.call-update) | async-done | bytes 1048592 | tf_op jit(solution)/shard_map/all_gather | solution.py:25
  786.2 10.4 %conditional.7 = (f32[512,768]{0,1:T(8,128)S(1)}) conditional(s32[]{:T(128)} %convert_element_type.9, () %tuple.51, (f32[1536,768]{0,1:T(8,128)}, f32[1,512,512]{1,0,2:T(1,128)}) %tuple.52), branch_computations={%region_9.10_spmd, %region_10.11_spmd} | conditional | flops 2415919104 | bytes 17825828 | solution.py:30
  786.4 6.1 copy.32
  792.5 4.1 fusion.10
  798.6 128.3 %all-gather.45.cloned.1.call-done = f32[8192,768]{0,1:T(8,128)} async-done(((f32[512,768]{0,1:T(8,128)}), f32[8192,768]{0,1:T(8,128)}) %all-gather.45.cloned.1.call-update) | async-done | bytes 25165840 | tf_op jit(solution)/shard_map/all_gather | solution.py:9
  926.9 26.7 %copy.59 = f32[96,8,16,512]{3,2,1,0:T(8,128)S(1)} copy(f32[96,8,16,512]{3,1,2,0:T(8,128)} %bitcast.60) | data formatting | bytes 50331648
  953.6 6.3 bitcast_reduce_fusion
  959.9 19.6 %all-gather.47.cloned.1.call-done = f32[1,1536,512]{1,2,0:T(8,128)} async-done(((f32[1,1536,32]{1,2,0:T(8,128)}), f32[1,1536,512]{1,2,0:T(8,128)}) %all-gather.47.cloned.1.call-update) | async-done | bytes 3145744 | tf_op jit(solution)/shard_map/all_gather | solution.py:24
  979.5 11.6 %subtract_select_fusion = f32[1536,768]{0,1:T(8,128)} fusion(f32[1536,768]{0,1:T(8,128)} %fusion.19, f32[512,768]{0,1:T(8,128)S(1)} %bitcast_reduce_fusion, f32[1,1536,512]{1,2,0:T(8,128)} %all-gather.47.cloned.1.call-done, pred[1536]{0:T(1024)(128)(4,1)S(1)} %fusion.25), kind=kOutput, calls=%fused_computation.18 | convolution fusion | flops 7250116608 | bytes 14157312 | tf_op jit(solution)/shard_map/dot_general | solution.py:13
  991.1 3.0 fusion.18
  994.1 6.0 copy.35
  (50 shorter events, 19.6 us)
Async XLA Ops:
  6.5 52.8 %all-gather.25.cloned.1.call-start = ((), (), s32[]{:S(2)}) async-start(), calls=%async_computation | async-start | bytes 1114112 | tf_op jit(solution)/shard_map/all_gather | solution.py:25
  8.2 190.6 %all-gather.27.cloned.1.call-start = ((), (), s32[]{:S(2)}) async-start(), calls=%async_computation.1 | async-start | bytes 26738688 | tf_op jit(solution)/shard_map/all_gather | solution.py:9
  62.2 1.1 copy-start.3
  62.2 189.4 %all-gather.29.cloned.1.call-start = ((), (), s32[]{:S(2)}) async-start(), calls=%async_computation.2 | async-start | bytes 3342336 | tf_op jit(solution)/shard_map/all_gather | solution.py:24
  64.2 234.8 %all-gather.31.cloned.1.call-start = ((), (), s32[]{:S(2)}) async-start(), calls=%async_computation.3 | async-start | bytes 1114112 | tf_op jit(solution)/shard_map/all_gather | solution.py:25
  65.0 377.5 %all-gather.33.cloned.1.call-start = ((), (), s32[]{:S(2)}) async-start(), calls=%async_computation.4 | async-start | bytes 26738688 | tf_op jit(solution)/shard_map/all_gather | solution.py:9
  301.0 194.1 %all-gather.35.cloned.1.call-start = ((), (), s32[]{:S(2)}) async-start(), calls=%async_computation.5 | async-start | bytes 3342336 | tf_op jit(solution)/shard_map/all_gather | solution.py:24
  301.6 241.1 %all-gather.37.cloned.1.call-start = ((), (), s32[]{:S(2)}) async-start(), calls=%async_computation.6 | async-start | bytes 1114112 | tf_op jit(solution)/shard_map/all_gather | solution.py:25
  302.4 383.6 %all-gather.39.cloned.1.call-start = ((), (), s32[]{:S(2)}) async-start(), calls=%async_computation.7 | async-start | bytes 26738688 | tf_op jit(solution)/shard_map/all_gather | solution.py:9
  544.5 194.2 %all-gather.41.cloned.1.call-start = ((), (), s32[]{:S(2)}) async-start(), calls=%async_computation.8 | async-start | bytes 3342336 | tf_op jit(solution)/shard_map/all_gather | solution.py:24
  545.2 241.0 %all-gather.43.cloned.1.call-start = ((), (), s32[]{:S(2)}) async-start(), calls=%async_computation.9 | async-start | bytes 1114112 | tf_op jit(solution)/shard_map/all_gather | solution.py:25
  546.0 380.9 %all-gather.45.cloned.1.call-start = ((), (), s32[]{:S(2)}) async-start(), calls=%async_computation.10 | async-start | bytes 26738688 | tf_op jit(solution)/shard_map/all_gather | solution.py:9
  786.4 6.1 copy-start
  798.0 181.5 %all-gather.47.cloned.1.call-start = ((), (), s32[]{:S(2)}) async-start(), calls=%async_computation.11 | async-start | bytes 3342336 | tf_op jit(solution)/shard_map/all_gather | solution.py:24
Sparse Core Ops, SparseCore 0:
  9.8 49.4 all-gather.24
  62.3 136.4 all-gather.26
  201.2 50.2 all-gather.28
  253.9 45.1 all-gather.30
  301.2 141.2 all-gather.32
  444.8 50.2 all-gather.34
  497.5 45.1 all-gather.36
  544.6 141.2 all-gather.38
  688.4 50.2 all-gather.40
  741.0 45.1 all-gather.42
  798.2 128.7 all-gather.44
  929.2 50.2 all-gather.46
